TPU v7x, 128 devices: a whole 4x4x4 slice. The times are simulated.
128 devices in a mesh: row: 8 (over x, y_lo), col: 16 (over z, y_hi, core).
Axes of the slice: x: 4, y: 4 (y_hi: 2, y_lo: 2; y = y_hi * 2 + y_lo), z: 4, core: 2. Of those that a mesh axis runs over, the one named last changes fastest.
Arguments:
- amplitudes: float32 [16, 16, 256, 256], P('row', 'col'), may hold values from -6 to 6
- coulomb: bfloat16 [16, 16, 256, 256], P('row'), may hold values from -6 to 6
- inner_list: int32 [16, 16, 8], P('row', 'col'), may hold values from 0 to 15, as said below
- inner_count: int32 [16, 16], P('row', 'col'), may hold values from 4 to 8
- reader_list: int32 [16, 16, 8], P('row'), may hold values from 0 to 15, as said below
- reader_count: int32 [16, 16], P('row'), may hold values from 4 to 8
- virtual_energy: float32 [256], replicated, may hold values from 0.5 to 2.5
- occupied_energy: float32 [16], replicated, may hold values from -1.5 to -0.3
Outputs:
- new_amplitudes: float32 [16, 16, 256, 256], P('row', 'col')
Inputs may be any that keep to these rules, and one draw needn't show every extreme that they name: `inner_list`: for each pair block the 8 entries are distinct orbitals; only the first inner_count of them are used. `reader_list`: for each pair block the 8 entries are distinct orbitals; only the first reader_count of them are used.
All inputs are finite; a program needn't handle non-finite values.
Results may differ from a plain program's by a relative error of at most 0.0015.
Values may be sent and summed in bfloat16 or wider, within the bound.
A program may use at most 64 MiB of HBM per device.

v0:
```python
import jax
import jax.numpy as jnp
from jax import lax
from jax.sharding import PartitionSpec as P

ITERS = 2
damping = 0.5
coupling = 0.03125


def on_device(
    amplitudes,
    coulomb,
    inner_list,
    inner_count,
    reader_list,
    reader_count,
    virtual_energy,
    occupied_energy,
):
    orb_rows = amplitudes.shape[0]
    orb_cols = amplitudes.shape[1]
    slot_count = inner_list.shape[2]
    row_start = lax.axis_index("row") * orb_rows
    col_start = lax.axis_index("col") * orb_cols
    occ_rows = lax.dynamic_slice_in_dim(occupied_energy, row_start, orb_rows, 0)
    occ_cols = lax.dynamic_slice_in_dim(occupied_energy, col_start, orb_cols, 0)
    virt_pair = virtual_energy[:, None] + virtual_energy[None, :]
    denominator = (
        virt_pair[None, None] - occ_rows[:, None, None, None] - occ_cols[None, :, None, None]
    )
    slot_iota = jnp.arange(slot_count, dtype=jnp.int32)
    row_iota = jnp.arange(orb_rows, dtype=jnp.int32)[:, None, None]
    col_iota = jnp.arange(orb_cols, dtype=jnp.int32)[None, :, None]
    inner_mask = (slot_iota < inner_count[..., None]).astype(jnp.bfloat16)[..., None, None]
    own_readers = lax.dynamic_slice_in_dim(reader_list, col_start, orb_cols, 1)
    own_reader_len = lax.dynamic_slice_in_dim(reader_count, col_start, orb_cols, 1)
    reader_mask = (slot_iota < own_reader_len[..., None]).astype(jnp.bfloat16)[..., None, None]
    coulomb_own = lax.dynamic_slice_in_dim(coulomb, col_start, orb_cols, 1).astype(jnp.float32)
    left_inner = coulomb[row_iota, inner_list]
    amp_state = amplitudes
    for sweep_index in range(ITERS):
        amp_half = amp_state.astype(jnp.bfloat16)
        amp_columns = lax.all_gather(amp_half, "row", axis=0, tiled=True)
        right_inner = amp_columns[inner_list, col_iota] * inner_mask
        coupled = jnp.einsum(
            "ijsab,ijsbc->ijac", left_inner, right_inner, preferred_element_type=jnp.float32
        ).astype(jnp.bfloat16)
        coupled_columns = lax.all_gather(coupled, "row", axis=0, tiled=True)
        coupled_rows = lax.all_to_all(
            coupled_columns, "col", split_axis=0, concat_axis=1, tiled=True
        )
        mirror = jnp.transpose(
            lax.dynamic_slice_in_dim(coupled_rows, row_start, orb_rows, 1), (1, 0, 3, 2)
        )
        right_reader = coupled_columns[own_readers, col_iota] * reader_mask
        amp_rows = lax.all_gather(amp_half, "col", axis=1, tiled=True)
        left_reader = amp_rows[row_iota, own_readers]
        quadratic = jnp.einsum(
            "ijsab,ijsbc->ijac", left_reader, right_reader, preferred_element_type=jnp.float32
        )
        residual = (
            coulomb_own
            + coupling * (coupled.astype(jnp.float32) + mirror.astype(jnp.float32))
            + coupling * coupling * quadratic
        )
        amp_state = damping * amp_state - residual / denominator
    return amp_state


def solution(mesh):
    return jax.shard_map(
        on_device,
        mesh=mesh,
        in_specs=(
            P("row", "col", None, None),
            P("row", None, None, None),
            P("row", "col", None),
            P("row", "col"),
            P("row", None, None),
            P("row", None),
            P(),
            P(),
        ),
        out_specs=P("row", "col", None, None),
        check_vma=False,
    )
```

profile of v0, /device:TPU:1, one launch (start us, length us, event | category | flops | bytes accessed | tf_op | source)
XLA Modules:
  0.0 391.9 jit_solution(14267644027346781398)
XLA Ops:
  6.5 1.8 convert_element_type.66
  8.4 0.8 copy.51
  9.2 0.7 broadcast_compare_fusion
  9.9 0.7 broadcast_add_fusion.1
  10.7 0.1 select_reduce_fusion
  11.0 0.9 fusion.67
  12.1 2.9 gather_fusion
  15.0 46.9 %all-gather.9.cloned.1.call-done = bf16[16,1,256,256]{3,2,1,0:T(8,128)(2,1)} async-done(((bf16[2,1,256,256]{3,2,1,0:T(8,128)(2,1)}), bf16[16,1,256,256]{3,2,1,0:T(8,128)(2,1)}) %all-gather.9.cloned.1.call-update) | async-done | bytes 2097168 | tf_op jit(solution)/shard_map/all_gather | solution.py:44
  61.9 3.6 gather_fusion.1
  65.5 3.1 fusion.41
  68.7 0.7 all-gather.11.cloned.1.call-update
  69.4 51.3 %all-gather.17.cloned.1.call-done = bf16[16,256,256]{2,1,0:T(8,128)(2,1)} async-done(((bf16[2,256,256]{2,1,0:T(8,128)(2,1)}), bf16[16,256,256]{2,1,0:T(8,128)(2,1)}) %all-gather.17.cloned.1.call-update) | async-done | bytes 2097168 | tf_op jit(solution)/shard_map/all_gather | solution.py:49
  120.6 8.7 %all-to-all-start = ((bf16[16,1,256,256]{3,2,1,0:T(8,128)(2,1)}), bf16[16,1,256,256]{3,2,1,0:T(8,128)(2,1)}, u32[]{:S(2)}, u32[]{:S(2)}) async-start(bf16[16,1,256,256]{3,2,1,0:T(8,128)(2,1)} %bitcast.127), calls=%async_computation | async-start | bytes 4194304 | tf_op jit(solution)/shard_map/all_to_all | solution.py:50
  129.3 0.7 dynamic_slice.21
  130.1 0.2 fusion.68
  130.7 2.0 gather_fusion.3
  132.7 57.3 %all-gather.11.cloned.1.call-done = bf16[2,16,256,256]{3,2,1,0:T(8,128)(2,1)} async-done(((bf16[2,1,256,256]{3,2,1,0:T(8,128)(2,1)}), bf16[2,16,256,256]{3,2,1,0:T(8,128)(2,1)}) %all-gather.11.cloned.1.call-update) | async-done | bytes 4194320 | tf_op jit(solution)/shard_map/all_gather | solution.py:57
  190.1 4.2 %gather_fusion.2 = bf16[16,256,256]{2,1,0:T(8,128)(2,1)} fusion(bf16[2,16,256,256]{3,2,1,0:T(8,128)(2,1)} %all-gather.11.cloned.1.call-done, s32[16]{0:T(128)S(1)} %reshape.182), kind=kCustom, calls=%fused_computation.2 | custom fusion | bytes 4194432 | tf_op jit(solution)/shard_map/gather | solution.py:58
  194.3 1.0 constant_dynamic-slice_fusion.2
  195.3 0.9 copy.67
  196.1 4.2 %fusion.85 = (bf16[2,1,256,256]{3,2,0,1:T(8,128)(2,1)}, f32[2,1,256,256]{3,2,0,1:T(8,128)}) fusion(f32[]{:T(128)} %bitcast.20, f32[2]{0:T(128)S(1)} %dynamic_slice.20, f32[256,256]{1,0:T(8,128)S(1)} %broadcast_add_fusion, bf16[2,8,256,256]{3,2,1,0:T(8,128)(2,1)} %bitcast.136, bf16[2,8,256,256]{3,2,1,0:T(8,128)(2,1)S(1)} %bitcast.135, ...), kind=kOutput, calls=%fused_computation.88 | convolution fusion | flops 539754496 | bytes 6553648 | tf_op jit(solution)/shard_map/ijsab,ijsbc->ijac/dot_general | solution.py:59
  200.4 47.1 %all-gather.13.cloned.1.call-done = bf16[16,1,256,256]{3,2,1,0:T(8,128)(2,1)} async-done(((bf16[2,1,256,256]{3,2,1,0:T(8,128)(2,1)}), bf16[16,1,256,256]{3,2,1,0:T(8,128)(2,1)}) %all-gather.13.cloned.1.call-update) | async-done | bytes 2097168 | tf_op jit(solution)/shard_map/all_gather | solution.py:44
  247.4 3.6 gather_fusion.4
  251.1 3.1 fusion.38
  254.2 0.5 all-gather.15.cloned.1.call-update
  254.8 51.4 %all-gather.19.cloned.1.call-done = bf16[16,256,256]{2,1,0:T(8,128)(2,1)} async-done(((bf16[2,256,256]{2,1,0:T(8,128)(2,1)}), bf16[16,256,256]{2,1,0:T(8,128)(2,1)}) %all-gather.19.cloned.1.call-update) | async-done | bytes 2097168 | tf_op jit(solution)/shard_map/all_gather | solution.py:49
  306.2 8.7 %all-to-all-start.1 = ((bf16[16,1,256,256]{3,2,1,0:T(8,128)(2,1)}), bf16[16,1,256,256]{3,2,1,0:T(8,128)(2,1)}, u32[]{:S(2)}, u32[]{:S(2)}) async-start(bf16[16,1,256,256]{3,2,1,0:T(8,128)(2,1)} %bitcast.129), calls=%async_computation.1 | async-start | bytes 4194304 | tf_op jit(solution)/shard_map/all_to_all | solution.py:50
  314.9 2.0 gather_fusion.6
  316.9 58.7 %all-gather.15.cloned.1.call-done = bf16[2,16,256,256]{3,2,0,1:T(8,128)(2,1)} async-done(((bf16[2,1,256,256]{3,2,0,1:T(8,128)(2,1)}), bf16[2,16,256,256]{3,2,0,1:T(8,128)(2,1)}) %all-gather.15.cloned.1.call-update) | async-done | bytes 4194320 | tf_op jit(solution)/shard_map/all_gather | solution.py:57
  375.6 4.2 %gather_fusion.5 = bf16[16,256,256]{2,1,0:T(8,128)(2,1)} fusion(bf16[2,16,256,256]{3,2,0,1:T(8,128)(2,1)} %all-gather.15.cloned.1.call-done, s32[16]{0:T(128)S(1)} %reshape.182), kind=kCustom, calls=%fused_computation.5 | custom fusion | bytes 4194432 | tf_op jit(solution)/shard_map/gather | solution.py:58
  379.8 1.0 constant_dynamic-slice_fusion
  380.9 4.1 %fusion.52 = f32[2,1,256,256]{3,2,1,0:T(8,128)} fusion(bf16[2,8,256,256]{3,2,1,0:T(8,128)(2,1)} %bitcast.134, bf16[2,8,256,256]{3,2,1,0:T(8,128)(2,1)S(1)} %bitcast.133, bf16[2,8]{1,0:T(2,128)(2,1)S(1)} %compare_convert_fusion, f32[2,1,256,256]{3,2,0,1:T(8,128)} %get-tuple-element.8, bf16[2,1,256,256]{2,3,0,1:T(8,128)(2,1)S(1)} %copy.68, ...), kind=kOutput, calls=%fused_computation.31 | convolution fusion | flops 539623424 | bytes 6291504 | tf_op jit(solution)/shard_map/ijsab,ijsbc->ijac/dot_general | solution.py:59
  (58 shorter events, 1.4 us)
Async XLA Ops:
  6.5 123.5 %copy-start = (s32[2,16]{1,0:T(2,128)S(1)}, s32[2,16]{1,0:T(2,128)}, u32[]{:S(2)}) copy-start(s32[2,16]{1,0:T(2,128)} %param.13) | copy-start | bytes 388
  6.5 55.4 %all-gather.9.cloned.1.call-start = ((), (), s32[]{:S(2)}) async-start(), calls=%async_computation.2 | async-start | bytes 2359296 | tf_op jit(solution)/shard_map/all_gather | solution.py:44
  8.3 112.3 %all-gather.17.cloned.1.call-start = ((), (), s32[]{:S(2)}) async-start(), calls=%async_computation.6 | async-start | bytes 2359296 | tf_op jit(solution)/shard_map/all_gather | solution.py:49
  12.0 2.9 copy-start.11
  14.9 50.6 %copy-start.3 = (bf16[16,256,256]{2,1,0:T(8,128)(2,1)}, bf16[16,256,256]{2,1,0:T(8,128)(2,1)S(1)}, u32[]{:S(2)}) copy-start(bf16[16,256,256]{2,1,0:T(8,128)(2,1)S(1)} %gather_fusion) | copy-start | bytes 6291460
  68.6 121.4 %all-gather.11.cloned.1.call-start = ((), (), s32[]{:S(2)}) async-start(), calls=%async_computation.3 | async-start | bytes 4456448 | tf_op jit(solution)/shard_map/all_gather | solution.py:57
  120.6 8.7 %copy-start.12 = (f32[16]{0:T(128)S(1)}, f32[16]{0:T(128)}, u32[]{:S(2)}) copy-start(f32[16]{0:T(128)} %param.15) | copy-start | bytes 196
  120.6 9.9 %copy-start.10 = (f32[256]{0:T(256)S(1)}, f32[256]{0:T(256)}, u32[]{:S(2)}) copy-start(f32[256]{0:T(256)} %param.14) | copy-start | bytes 3076
  120.6 10.0 %copy-start.1 = (bf16[16,256,256]{2,1,0:T(8,128)(2,1)S(1)}, bf16[16,256,256]{2,1,0:T(8,128)(2,1)}, u32[]{:S(2)}) copy-start(bf16[16,256,256]{2,1,0:T(8,128)(2,1)} %all-gather.17.cloned.1.call-done) | copy-start | bytes 6291460
  120.6 73.7 %all-to-all-start = ((bf16[16,1,256,256]{3,2,1,0:T(8,128)(2,1)}), bf16[16,1,256,256]{3,2,1,0:T(8,128)(2,1)}, u32[]{:S(2)}, u32[]{:S(2)}) async-start(bf16[16,1,256,256]{3,2,1,0:T(8,128)(2,1)} %bitcast.127), calls=%async_computation | async-start | bytes 4194304 | tf_op jit(solution)/shard_map/all_to_all | solution.py:50
  129.3 118.2 %all-gather.13.cloned.1.call-start = ((), (), s32[]{:S(2)}) async-start(), calls=%async_computation.4 | async-start | bytes 2359296 | tf_op jit(solution)/shard_map/all_gather | solution.py:44
  132.7 63.4 %copy-start.6 = (bf16[16,256,256]{2,1,0:T(8,128)(2,1)S(1)}, bf16[16,256,256]{2,1,0:T(8,128)(2,1)}, u32[]{:S(2)}) copy-start(bf16[16,256,256]{2,1,0:T(8,128)(2,1)} %gather_fusion.3) | copy-start | bytes 6291460
  132.7 63.4 %copy-start.7 = (f32[2,1,256,256]{3,2,1,0:T(8,128)S(1)}, f32[2,1,256,256]{3,2,1,0:T(8,128)}, u32[]{:S(2)}) copy-start(f32[2,1,256,256]{3,2,1,0:T(8,128)} %param.8) | copy-start | bytes 1572868
  132.7 63.4 %copy-start.8 = (bf16[2,256,256]{2,1,0:T(8,128)(2,1)S(1)}, bf16[2,256,256]{2,1,0:T(8,128)(2,1)}, u32[]{:S(2)}) copy-start(bf16[2,256,256]{2,1,0:T(8,128)(2,1)} %fusion.41) | copy-start | bytes 786436
  200.3 50.7 %copy-start.4 = (bf16[16,256,256]{2,1,0:T(8,128)(2,1)S(1)}, bf16[16,256,256]{2,1,0:T(8,128)(2,1)}, u32[]{:S(2)}) copy-start(bf16[16,256,256]{2,1,0:T(8,128)(2,1)} %copy-done.3) | copy-start | bytes 6291460
  200.3 105.9 %all-gather.19.cloned.1.call-start = ((), (), s32[]{:S(2)}) async-start(), calls=%async_computation.7 | async-start | bytes 2359296 | tf_op jit(solution)/shard_map/all_gather | solution.py:49
  254.2 121.4 %all-gather.15.cloned.1.call-start = ((), (), s32[]{:S(2)}) async-start(), calls=%async_computation.5 | async-start | bytes 4456448 | tf_op jit(solution)/shard_map/all_gather | solution.py:57
  306.2 8.7 %copy-start.2 = (bf16[16,256,256]{2,1,0:T(8,128)(2,1)S(1)}, bf16[16,256,256]{2,1,0:T(8,128)(2,1)}, u32[]{:S(2)}) copy-start(bf16[16,256,256]{2,1,0:T(8,128)(2,1)} %all-gather.19.cloned.1.call-done) | copy-start | bytes 6291460
  306.2 73.6 %all-to-all-start.1 = ((bf16[16,1,256,256]{3,2,1,0:T(8,128)(2,1)}), bf16[16,1,256,256]{3,2,1,0:T(8,128)(2,1)}, u32[]{:S(2)}, u32[]{:S(2)}) async-start(bf16[16,1,256,256]{3,2,1,0:T(8,128)(2,1)} %bitcast.129), calls=%async_computation.1 | async-start | bytes 4194304 | tf_op jit(solution)/shard_map/all_to_all | solution.py:50
  316.9 64.1 %copy-start.5 = (bf16[16,256,256]{2,1,0:T(8,128)(2,1)S(1)}, bf16[16,256,256]{2,1,0:T(8,128)(2,1)}, u32[]{:S(2)}) copy-start(bf16[16,256,256]{2,1,0:T(8,128)(2,1)} %gather_fusion.6) | copy-start | bytes 6291460
  316.9 64.1 %copy-start.9 = (bf16[2,256,256]{2,1,0:T(8,128)(2,1)S(1)}, bf16[2,256,256]{2,1,0:T(8,128)(2,1)}, u32[]{:S(2)}) copy-start(bf16[2,256,256]{2,1,0:T(8,128)(2,1)} %fusion.38) | copy-start | bytes 786436
Sparse Core Ops, SparseCore 0:
  9.0 52.8 all-gather.8
  68.7 51.8 all-gather.16
  123.1 66.9 all-gather.10
  200.4 46.9 all-gather.12
  254.3 51.8 all-gather.18
  308.5 67.0 all-gather.14
where the time goes:
time: 393 us; the launch traced here: 392 us
  waiting for transfers between devices  314 us (80%)
  local copies, waits for them, and re-layouts  27.8 us (7%)
  starting transfers between devices  17.5 us (4%)
  matrix products  14.5 us (4%)
  between operations  13.6 us (3%)
  other arithmetic  4.55 us (1%)
    all_gather x2, waiting for transfers between devices, on_device(): amp_rows = lax.all_gather(amp_half, 'col', axis=1, tiled=True)  116 us
    all_gather x2, waiting for transfers between devices, on_device(): coupled_columns = lax.all_gather(coupled, 'row', axis=0, tiled=True)  103 us
    all_gather x2, waiting for transfers between devices, on_device(): amp_columns = lax.all_gather(amp_half, 'row', axis=0, tiled=True)  93.9 us
    all_to_all x2, starting transfers between devices, on_device(): lax.all_to_all(coupled_columns, 'col', split_axis=0, concat_axis=1, tiled...  17.3 us
    gather x2, local copies, waits for them, and re-layouts, on_device(): left_reader = amp_rows[row_iota, own_readers]  8.44 us
    dot_general x2, matrix products, on_device(): jnp.einsum('ijsab,ijsbc->ijac', left_reader, right_reader, preferred_elem...  8.3 us
  transfers between devices with their start and end apart: 8, of which 6 were waited for; matrix products, arithmetic and copies ran while one was open for 5% of the time, Pallas kernels for 0%

commit v1 on v0

--- a/solution.py
+++ b/solution.py
@@ -54,7 +54,9 @@
             lax.dynamic_slice_in_dim(coupled_rows, row_start, orb_rows, 1), (1, 0, 3, 2)
         )
         right_reader = coupled_columns[own_readers, col_iota] * reader_mask
-        amp_rows = lax.all_gather(amp_half, "col", axis=1, tiled=True)
+        amp_rows = jnp.concatenate(
+            lax.all_to_all(jnp.stack([amp_half] * lax.axis_size("col")), "col", 0, 0), axis=1
+        )
         left_reader = amp_rows[row_iota, own_readers]
         quadratic = jnp.einsum(
             "ijsab,ijsbc->ijac", left_reader, right_reader, preferred_element_type=jnp.float32

time: 393 us -> 373 us (0.949)
  waiting for transfers between devices: 314 us -> 275 us
  starting transfers between devices: 17.5 us -> 32.6 us
    all_gather x2 -> x0, waiting for transfers between devices: 116 us -> none  [on_device(): amp_rows = lax.all_gather(amp_half, 'col', axis=1, tiled=True)]
    all_to_all x0 -> x2, waiting for transfers between devices: none -> 74.6 us  [on_device(): lax.all_to_all(jnp.stack([amp_half] * lax.axis_size('col')), 'col', 0, 0)]
    all_gather x2, waiting for transfers between devices: 103 us -> 44.6 us  [on_device(): coupled_columns = lax.all_gather(coupled, 'row', axis=0, tiled=True)]
    all_to_all x2, waiting for transfers between devices: 0.01 us -> 42.7 us  [on_device(): lax.all_to_all(coupled_columns, 'col', split_axis=0, concat_axis=1, tiled...]
    all_gather x2, waiting for transfers between devices: 93.9 us -> 113 us  [on_device(): amp_columns = lax.all_gather(amp_half, 'row', axis=0, tiled=True)]
    all_to_all x0 -> x2, starting transfers between devices: none -> 14.9 us  [on_device(): lax.all_to_all(jnp.stack([amp_half] * lax.axis_size('col')), 'col', 0, 0)]
    another operation x2 -> x4, local copies, waits for them, and re-layouts: 1.94 us -> 6.82 us  [the longest x2 4.89 us: on_device(): jnp.stack([amp_half] * lax.axis_size('col'))]
  transfers between devices with their start and end apart: 8 -> 8, of which waited for: 6 -> 8; matrix products, arithmetic and copies ran while one was open for 5% -> 10% of each run, Pallas kernels for 0% -> 0%
where the time goes in v1:
time: 373 us; the launch traced here: 372 us
  waiting for transfers between devices  275 us (74%)
  starting transfers between devices  32.6 us (9%)
  local copies, waits for them, and re-layouts  31.5 us (8%)
  matrix products  14.7 us (4%)
  between operations  13.3 us (4%)
  other arithmetic  4.31 us (1%)
    all_gather x2, waiting for transfers between devices, on_device(): amp_columns = lax.all_gather(amp_half, 'row', axis=0, tiled=True)  113 us
    all_to_all x2, waiting for transfers between devices, on_device(): lax.all_to_all(jnp.stack([amp_half] * lax.axis_size('col')), 'col', 0, 0)  74.6 us
    all_gather x2, waiting for transfers between devices, on_device(): coupled_columns = lax.all_gather(coupled, 'row', axis=0, tiled=True)  44.6 us
    all_to_all x2, waiting for transfers between devices, on_device(): lax.all_to_all(coupled_columns, 'col', split_axis=0, concat_axis=1, tiled...  42.7 us
    all_to_all x2, starting transfers between devices, on_device(): lax.all_to_all(coupled_columns, 'col', split_axis=0, concat_axis=1, tiled...  17.6 us
    all_to_all x2, starting transfers between devices, on_device(): lax.all_to_all(jnp.stack([amp_half] * lax.axis_size('col')), 'col', 0, 0)  14.9 us
    gather x2, local copies, waits for them, and re-layouts, on_device(): left_reader = amp_rows[row_iota, own_readers]  8.72 us
    dot_general x2, matrix products, on_device(): jnp.einsum('ijsab,ijsbc->ijac', left_reader, right_reader, preferred_elem...  8.5 us
  transfers between devices with their start and end apart: 8, of which 8 were waited for; matrix products, arithmetic and copies ran while one was open for 10% of the time, Pallas kernels for 0%

profile of v1, /device:TPU:1, one launch (start us, length us, event | category | flops | bytes accessed | tf_op | source)
XLA Modules:
  0.0 371.9 jit_solution(5672936811255771432)
XLA Ops:
  6.5 1.8 convert_element_type.70
  8.3 1.1 convert_bitcast_fusion.4
  9.4 2.4 stack.4
  11.9 9.6 %all-to-all-start.1 = ((bf16[16,2,1,256,256]{4,3,2,1,0:T(8,128)(2,1)}), bf16[16,2,1,256,256]{4,3,2,1,0:T(8,128)(2,1)}, u32[]{:S(2)}, u32[]{:S(2)}) async-start(bf16[16,2,1,256,256]{4,3,2,1,0:T(8,128)(2,1)} %stack.4), calls=%async_computation.1 | async-start | bytes 8388608 | tf_op jit(solution)/shard_map/all_to_all | solution.py:58
  21.8 0.2 fusion.67
  22.4 2.9 gather_fusion
  25.4 56.2 %all-gather.7.cloned.1.call-done = bf16[16,1,256,256]{3,2,1,0:T(8,128)(2,1)} async-done(((bf16[2,1,256,256]{3,2,1,0:T(8,128)(2,1)}), bf16[16,1,256,256]{3,2,1,0:T(8,128)(2,1)}) %all-gather.7.cloned.1.call-update) | async-done | bytes 2097168 | tf_op jit(solution)/shard_map/all_gather | solution.py:44
  81.6 3.6 gather_fusion.1
  85.2 3.1 fusion.41
  88.3 36.4 %all-to-all-done.1 = bf16[16,2,1,256,256]{4,3,2,1,0:T(8,128)(2,1)} async-done(((bf16[16,2,1,256,256]{4,3,2,1,0:T(8,128)(2,1)}), bf16[16,2,1,256,256]{4,3,2,1,0:T(8,128)(2,1)}, u32[]{:S(2)}, u32[]{:S(2)}) %all-to-all-start.1) | async-done | bytes 4194336 | tf_op jit(solution)/shard_map/all_to_all | solution.py:58
  124.6 22.6 %all-gather.11.cloned.1.call-done = bf16[16,256,256]{2,1,0:T(8,128)(2,1)} async-done(((bf16[2,256,256]{2,1,0:T(8,128)(2,1)}), bf16[16,256,256]{2,1,0:T(8,128)(2,1)}) %all-gather.11.cloned.1.call-update) | async-done | bytes 2097168 | tf_op jit(solution)/shard_map/all_gather | solution.py:49
  147.3 8.8 %all-to-all-start = ((bf16[16,1,256,256]{3,2,1,0:T(8,128)(2,1)}), bf16[16,1,256,256]{3,2,1,0:T(8,128)(2,1)}, u32[]{:S(2)}, u32[]{:S(2)}) async-start(bf16[16,1,256,256]{3,2,1,0:T(8,128)(2,1)} %bitcast.138), calls=%async_computation | async-start | bytes 4194304 | tf_op jit(solution)/shard_map/all_to_all | solution.py:50
  156.6 0.7 dynamic_slice.21
  157.5 4.4 %gather_fusion.2 = bf16[16,256,256]{2,1,0:T(8,128)(2,1)} fusion(bf16[2,16,256,256]{3,2,0,1:T(8,128)(2,1)} %bitcast.15, s32[16]{0:T(128)S(1)} %reshape.204), kind=kCustom, calls=%fused_computation.2 | custom fusion | bytes 4194432 | tf_op jit(solution)/shard_map/gather | solution.py:60
  161.9 2.0 gather_fusion.3
  163.9 20.7 %all-to-all-done = bf16[16,1,256,256]{3,2,1,0:T(8,128)(2,1)} async-done(((bf16[16,1,256,256]{3,2,1,0:T(8,128)(2,1)}), bf16[16,1,256,256]{3,2,1,0:T(8,128)(2,1)}, u32[]{:S(2)}, u32[]{:S(2)}) %all-to-all-start) | async-done | bytes 2097184 | tf_op jit(solution)/shard_map/all_to_all | solution.py:50
  184.5 1.0 constant_dynamic-slice_fusion.2
  185.7 3.9 %fusion.58 = f32[2,1,256,256]{3,2,0,1:T(8,128)S(1)} fusion(bf16[2,8,256,256]{3,2,1,0:T(8,128)(2,1)} %bitcast.146, bf16[2,8,256,256]{3,2,1,0:T(8,128)(2,1)} %bitcast.147, bf16[2,8]{1,0:T(2,128)(2,1)S(1)} %compare_convert_fusion, f32[2,1,256,256]{3,2,1,0:T(8,128)S(1)} %copy-done.3, bf16[2,1,256,256]{2,3,0,1:T(8,128)(2,1)S(1)} %copy.67, ...), kind=kOutput, calls=%fused_computation.33 | convolution fusion | flops 539623424 | bytes 6291504 | tf_op jit(solution)/shard_map/ijsab,ijsbc->ijac/dot_general | solution.py:61
  189.6 0.7 convert_bitcast_fusion.3
  190.3 2.4 stack.5
  192.8 5.3 %all-to-all-start.3 = ((bf16[16,2,1,256,256]{4,3,2,1,0:T(8,128)(2,1)}), bf16[16,2,1,256,256]{4,3,2,1,0:T(8,128)(2,1)}, u32[]{:S(2)}, u32[]{:S(2)}) async-start(bf16[16,2,1,256,256]{4,3,2,1,0:T(8,128)(2,1)} %stack.5), calls=%async_computation.3 | async-start | bytes 8388608 | tf_op jit(solution)/shard_map/all_to_all | solution.py:58
  198.1 57.3 %all-gather.9.cloned.1.call-done = bf16[16,1,256,256]{3,2,1,0:T(8,128)(2,1)} async-done(((bf16[2,1,256,256]{3,2,1,0:T(8,128)(2,1)}), bf16[16,1,256,256]{3,2,1,0:T(8,128)(2,1)}) %all-gather.9.cloned.1.call-update) | async-done | bytes 2097168 | tf_op jit(solution)/shard_map/all_gather | solution.py:44
  255.4 3.6 gather_fusion.4
  259.0 3.1 fusion.38
  262.1 38.3 %all-to-all-done.3 = bf16[16,2,1,256,256]{4,3,2,1,0:T(8,128)(2,1)} async-done(((bf16[16,2,1,256,256]{4,3,2,1,0:T(8,128)(2,1)}), bf16[16,2,1,256,256]{4,3,2,1,0:T(8,128)(2,1)}, u32[]{:S(2)}, u32[]{:S(2)}) %all-to-all-start.3) | async-done | bytes 4194336 | tf_op jit(solution)/shard_map/all_to_all | solution.py:58
  300.4 21.9 %all-gather.13.cloned.1.call-done = bf16[16,256,256]{2,1,0:T(8,128)(2,1)} async-done(((bf16[2,256,256]{2,1,0:T(8,128)(2,1)}), bf16[16,256,256]{2,1,0:T(8,128)(2,1)}) %all-gather.13.cloned.1.call-update) | async-done | bytes 2097168 | tf_op jit(solution)/shard_map/all_gather | solution.py:49
  322.3 8.8 %all-to-all-start.2 = ((bf16[16,1,256,256]{3,2,1,0:T(8,128)(2,1)}), bf16[16,1,256,256]{3,2,1,0:T(8,128)(2,1)}, u32[]{:S(2)}, u32[]{:S(2)}) async-start(bf16[16,1,256,256]{3,2,1,0:T(8,128)(2,1)} %bitcast.140), calls=%async_computation.2 | async-start | bytes 4194304 | tf_op jit(solution)/shard_map/all_to_all | solution.py:50
  331.2 4.4 %gather_fusion.5 = bf16[16,256,256]{2,1,0:T(8,128)(2,1)} fusion(bf16[2,16,256,256]{3,2,0,1:T(8,128)(2,1)} %bitcast.35, s32[16]{0:T(128)S(1)} %reshape.204), kind=kCustom, calls=%fused_computation.5 | custom fusion | bytes 4194432 | tf_op jit(solution)/shard_map/gather | solution.py:60
  335.5 2.0 gather_fusion.6
  337.6 22.1 %all-to-all-done.2 = bf16[16,1,256,256]{3,2,1,0:T(8,128)(2,1)} async-done(((bf16[16,1,256,256]{3,2,1,0:T(8,128)(2,1)}), bf16[16,1,256,256]{3,2,1,0:T(8,128)(2,1)}, u32[]{:S(2)}, u32[]{:S(2)}) %all-to-all-start.2) | async-done | bytes 2097184 | tf_op jit(solution)/shard_map/all_to_all | solution.py:50
  359.6 1.0 constant_dynamic-slice_fusion
  360.7 4.6 %fusion.52 = f32[2,1,256,256]{3,2,1,0:T(8,128)} fusion(bf16[2,8,256,256]{3,2,1,0:T(8,128)(2,1)} %bitcast.144, bf16[2,8,256,256]{3,2,1,0:T(8,128)(2,1)} %bitcast.145, bf16[2,8]{1,0:T(2,128)(2,1)S(1)} %compare_convert_fusion, f32[2,1,256,256]{3,2,0,1:T(8,128)S(1)} %fusion.58, bf16[2,1,256,256]{2,3,0,1:T(8,128)(2,1)S(1)} %copy.68, ...), kind=kOutput, calls=%fused_computation.31 | convolution fusion | flops 539623424 | bytes 6291504 | tf_op jit(solution)/shard_map/ijsab,ijsbc->ijac/dot_general | solution.py:61
  (58 shorter events, 1.9 us)
Async XLA Ops:
  6.5 149.8 %copy-start = (s32[2,16]{1,0:T(2,128)S(1)}, s32[2,16]{1,0:T(2,128)}, u32[]{:S(2)}) copy-start(s32[2,16]{1,0:T(2,128)} %param.13) | copy-start | bytes 388
  6.5 75.0 %all-gather.7.cloned.1.call-start = ((), (), s32[]{:S(2)}) async-start(), calls=%async_computation.4 | async-start | bytes 2359296 | tf_op jit(solution)/shard_map/all_gather | solution.py:44
  11.9 9.6 %copy-start.7 = (s32[2,1,8]{2,1,0:T(1,128)S(1)}, s32[2,1,8]{2,1,0:T(1,128)}, u32[]{:S(2)}) copy-start(s32[2,1,8]{2,1,0:T(1,128)} %param.10) | copy-start | bytes 196
  11.9 9.9 %copy-start.8 = (s32[2,16,8]{1,2,0:T(8,128)S(1)}, s32[2,16,8]{1,2,0:T(8,128)}, u32[]{:S(2)}) copy-start(s32[2,16,8]{1,2,0:T(8,128)} %param.12) | copy-start | bytes 3076
  11.9 112.8 %all-to-all-start.1 = ((bf16[16,2,1,256,256]{4,3,2,1,0:T(8,128)(2,1)}), bf16[16,2,1,256,256]{4,3,2,1,0:T(8,128)(2,1)}, u32[]{:S(2)}, u32[]{:S(2)}) async-start(bf16[16,2,1,256,256]{4,3,2,1,0:T(8,128)(2,1)} %stack.4), calls=%async_computation.1 | async-start | bytes 8388608 | tf_op jit(solution)/shard_map/all_to_all | solution.py:58
  21.4 125.8 %all-gather.11.cloned.1.call-start = ((), (), s32[]{:S(2)}) async-start(), calls=%async_computation.6 | async-start | bytes 2359296 | tf_op jit(solution)/shard_map/all_gather | solution.py:49
  22.4 2.9 copy-start.10
  25.3 59.9 %copy-start.4 = (bf16[16,256,256]{2,1,0:T(8,128)(2,1)}, bf16[16,256,256]{2,1,0:T(8,128)(2,1)S(1)}, u32[]{:S(2)}) copy-start(bf16[16,256,256]{2,1,0:T(8,128)(2,1)S(1)} %gather_fusion) | copy-start | bytes 6291460
  147.3 9.3 %copy-start.11 = (f32[16]{0:T(128)S(1)}, f32[16]{0:T(128)}, u32[]{:S(2)}) copy-start(f32[16]{0:T(128)} %param.15) | copy-start | bytes 196
  147.3 10.1 %copy-start.9 = (f32[256]{0:T(256)S(1)}, f32[256]{0:T(256)}, u32[]{:S(2)}) copy-start(f32[256]{0:T(256)} %param.14) | copy-start | bytes 3076
  147.3 37.2 %all-to-all-start = ((bf16[16,1,256,256]{3,2,1,0:T(8,128)(2,1)}), bf16[16,1,256,256]{3,2,1,0:T(8,128)(2,1)}, u32[]{:S(2)}, u32[]{:S(2)}) async-start(bf16[16,1,256,256]{3,2,1,0:T(8,128)(2,1)} %bitcast.138), calls=%async_computation | async-start | bytes 4194304 | tf_op jit(solution)/shard_map/all_to_all | solution.py:50
  156.1 99.3 %all-gather.9.cloned.1.call-start = ((), (), s32[]{:S(2)}) async-start(), calls=%async_computation.5 | async-start | bytes 2359296 | tf_op jit(solution)/shard_map/all_gather | solution.py:44
  157.5 4.4 %copy-start.1 = (bf16[16,256,256]{2,1,0:T(8,128)(2,1)S(1)}, bf16[16,256,256]{2,1,0:T(8,128)(2,1)}, u32[]{:S(2)}) copy-start(bf16[16,256,256]{2,1,0:T(8,128)(2,1)} %all-gather.11.cloned.1.call-done) | copy-start | bytes 6291460
  161.9 23.8 %copy-start.3 = (f32[2,1,256,256]{3,2,1,0:T(8,128)S(1)}, f32[2,1,256,256]{3,2,1,0:T(8,128)}, u32[]{:S(2)}) copy-start(f32[2,1,256,256]{3,2,1,0:T(8,128)} %param.8) | copy-start | bytes 1572868
  192.8 107.6 %all-to-all-start.3 = ((bf16[16,2,1,256,256]{4,3,2,1,0:T(8,128)(2,1)}), bf16[16,2,1,256,256]{4,3,2,1,0:T(8,128)(2,1)}, u32[]{:S(2)}, u32[]{:S(2)}) async-start(bf16[16,2,1,256,256]{4,3,2,1,0:T(8,128)(2,1)} %stack.5), calls=%async_computation.3 | async-start | bytes 8388608 | tf_op jit(solution)/shard_map/all_to_all | solution.py:58
  198.1 60.9 %copy-start.5 = (bf16[16,256,256]{2,1,0:T(8,128)(2,1)S(1)}, bf16[16,256,256]{2,1,0:T(8,128)(2,1)}, u32[]{:S(2)}) copy-start(bf16[16,256,256]{2,1,0:T(8,128)(2,1)} %copy-done.4) | copy-start | bytes 6291460
  198.1 124.3 %all-gather.13.cloned.1.call-start = ((), (), s32[]{:S(2)}) async-start(), calls=%async_computation.7 | async-start | bytes 2359296 | tf_op jit(solution)/shard_map/all_gather | solution.py:49
  322.3 37.3 %all-to-all-start.2 = ((bf16[16,1,256,256]{3,2,1,0:T(8,128)(2,1)}), bf16[16,1,256,256]{3,2,1,0:T(8,128)(2,1)}, u32[]{:S(2)}, u32[]{:S(2)}) async-start(bf16[16,1,256,256]{3,2,1,0:T(8,128)(2,1)} %bitcast.140), calls=%async_computation.2 | async-start | bytes 4194304 | tf_op jit(solution)/shard_map/all_to_all | solution.py:50
  331.2 4.4 %copy-start.2 = (bf16[16,256,256]{2,1,0:T(8,128)(2,1)S(1)}, bf16[16,256,256]{2,1,0:T(8,128)(2,1)}, u32[]{:S(2)}) copy-start(bf16[16,256,256]{2,1,0:T(8,128)(2,1)} %all-gather.13.cloned.1.call-done) | copy-start | bytes 6291460
  335.5 25.2 %copy-start.6 = (bf16[2,256,256]{2,1,0:T(8,128)(2,1)S(1)}, bf16[2,256,256]{2,1,0:T(8,128)(2,1)}, u32[]{:S(2)}) copy-start(bf16[2,256,256]{2,1,0:T(8,128)(2,1)} %fusion.38) | copy-start | bytes 786436
Sparse Core Ops, SparseCore 0:
  9.0 72.5 all-gather.6
  88.4 58.8 all-gather.10
  190.5 64.8 all-gather.8
  262.2 60.0 all-gather.12
